TPU v7x, 32 devices: a whole 2x2x4 slice. The times are simulated.
32 devices in a mesh: row: 8 (over y, x, core), col: 4 (over z).
Axes of the slice: x: 2, y: 2, z: 4, core: 2. Of those that a mesh axis runs over, the one named last changes fastest.
Arguments:
- density: bfloat16 [4096, 4096], P('row', 'col'), as said below
- pattern: int32 [64, 64], P('row', 'col'), may hold values from 0 to 1, as said below
Outputs:
- updated: bfloat16 [4096, 4096], P('row', 'col')
- occupations: float32 [2], replicated
Inputs may be any that keep to these rules, and one draw needn't show every extreme that they name: pattern is symmetric, every diagonal block is 1. density is exactly symmetric and zero wherever pattern is 0.
All inputs are finite; a program needn't handle non-finite values.
Results may differ from a plain program's by a relative error of at most 0.0015.
Values may be sent and summed in bfloat16 or wider, within the bound.
A program may use at most 64 MiB of HBM per device.

v0:
```python
import jax
import jax.numpy as jnp
from jax import lax
from jax.sharding import PartitionSpec as P

BLK = 64


def expand_blocks(block_mask, width):
    block_rows, block_cols = block_mask.shape
    grid = jnp.broadcast_to(
        block_mask.astype(jnp.float32)[:, None, :, None], (block_rows, width, block_cols, width)
    )
    return grid.reshape(block_rows * width, block_cols * width)


def body(density, pattern):
    slab_rows, slab_cols = density.shape
    cell_mask = expand_blocks(pattern, BLK)
    column_panel = lax.all_gather(density, "row", axis=0, tiled=True)
    row_offset = lax.axis_index("row") * slab_rows
    col_offset = lax.axis_index("col") * slab_cols
    global_rows = row_offset + lax.iota(jnp.int32, slab_rows)
    global_cols = col_offset + lax.iota(jnp.int32, slab_cols)
    on_diagonal = global_rows[:, None] == global_cols[None, :]
    density_wide = density.astype(jnp.float32)
    trace_p_part = jnp.sum(jnp.where(on_diagonal, density_wide, 0.0))
    square = jnp.dot(
        lax.all_gather(density, "col", axis=1, tiled=True),
        column_panel,
        preferred_element_type=jnp.float32,
    )
    square = square * cell_mask
    trace_c_part = jnp.sum(jnp.where(on_diagonal, square, 0.0))
    trace_p, trace_c = lax.psum((trace_p_part, trace_c_part), ("row", "col"))
    order_total = slab_rows * lax.axis_size("row")
    take_square = trace_p > 1.0 * order_total
    updated = jnp.where(take_square, square, cell_mask * (2.0 * density_wide - square))
    trace_new = jnp.where(take_square, trace_c, 2.0 * trace_p - trace_c)
    occupations = jnp.stack([trace_p, trace_new]) / order_total
    return (updated.astype(jnp.bfloat16), occupations)


def solution(mesh):
    placed = (P("row", "col"), P("row", "col"))
    return jax.shard_map(
        body, mesh=mesh, in_specs=placed, out_specs=(P("row", "col"), P()), check_vma=False
    )
```

profile of v0, /device:TPU:0, one launch (start us, length us, event | category | flops | bytes accessed | tf_op | source)
XLA Modules:
  0.0 212.4 jit_solution(5599611315656936817)
XLA Ops:
  7.2 0.0 copy-start.1
  7.2 0.0 all-gather.3.cloned.1.call-start
  7.2 0.7 all-gather.3.cloned.1.call-update
  7.9 0.0 all-gather.5.cloned.1.call-start
  8.0 0.7 all-gather.5.cloned.1.call-update
  8.7 0.0 copy-done.1
  8.7 2.3 %broadcast_in_dim.14 = f32[8,64,16,64]{3,2,1,0:T(8,128)} broadcast(f32[8,16]{1,0:T(8,128)S(1)} %convert_element_type.10), dimensions={0,2} | broadcast | bytes 2097664 | tf_op jit(solution)/shard_map/broadcast_in_dim | solution.py:11
  11.0 0.0 copy-start
  11.0 3.6 %reshape.16 = f32[512,1024]{1,0:T(8,128)S(1)} reshape(f32[8,64,16,64]{3,2,1,0:T(8,128)} %broadcast_in_dim.14) | data formatting | bytes 4194304 | tf_op jit(solution)/shard_map/reshape | solution.py:14
  14.6 78.5 %all-gather.3.cloned.1.call-done = bf16[512,4096]{1,0:T(8,128)(2,1)} async-done(((bf16[512,1024]{1,0:T(8,128)(2,1)}), bf16[512,4096]{1,0:T(8,128)(2,1)}) %all-gather.3.cloned.1.call-update) | async-done | bytes 4194320 | tf_op jit(solution)/shard_map/all_gather | solution.py:29
  93.1 54.8 %all-gather.5.cloned.1.call-done = bf16[4096,1024]{1,0:T(8,128)(2,1)} async-done(((bf16[512,1024]{1,0:T(8,128)(2,1)}), bf16[4096,1024]{1,0:T(8,128)(2,1)}) %all-gather.5.cloned.1.call-update) | async-done | bytes 8388624 | tf_op jit(solution)/shard_map/all_gather | solution.py:20
  147.9 0.0 copy-done
  147.9 11.1 %fusion.5 = (f32[]{:T(128)}, f32[]{:T(128)}, f32[512,1024]{1,0:T(8,128)}) fusion(f32[512,1024]{1,0:T(8,128)S(1)} %reshape.16, s32[1024]{0:T(1024)S(1)} %iota_add_fusion, s32[512]{0:T(512)S(1)} %iota_add_fusion.1, bf16[512,1024]{1,0:T(8,128)(2,1)S(1)} %copy-done, bf16[512,4096]{1,0:T(8,128)(2,1)} %all-gather.3.cloned.1.call-done, ...), kind=kOutput, calls=%fused_computation.8 | convolution fusion | flops 4298637312 | bytes 17831944 | tf_op jit(solution)/shard_map/dot_general | solution.py:28
  159.0 39.6 %all-reduce = (f32[]{:T(128)}, f32[]{:T(128)}) all-reduce(f32[]{:T(128)} %get-tuple-element.3, f32[]{:T(128)} %get-tuple-element.2), channel_id=1, replica_groups=mesh['row'=8,'col'=4] {'row','col'}, use_global_device_ids=true, to_apply=%region_1.2 | all-reduce | flops 2 | bytes 16 | tf_op jit(solution)/shard_map/psum | solution.py:35
  201.2 3.2 %fusion.3 = bf16[512,1024]{1,0:T(8,128)(2,1)} fusion(f32[512,1024]{1,0:T(8,128)S(1)} %reshape.16, bf16[512,1024]{1,0:T(8,128)(2,1)S(1)} %copy-done, f32[512,1024]{1,0:T(8,128)} %get-tuple-element.6, pred[]{:T(512)S(6)} %gt.3), kind=kLoop, calls=%fused_computation.6 | loop fusion | flops 3670016 | bytes 6291457 | tf_op jit(solution)/shard_map/convert_element_type | solution.py:41
  204.3 1.2 maximum_multiply_fusion
  (3 shorter events, 0.0 us)
Async XLA Ops:
  7.2 1.5 copy-start.1
  7.2 85.9 %all-gather.3.cloned.1.call-start = ((), (), s32[]{:S(2)}) async-start(), calls=%async_computation | async-start | bytes 5242880 | tf_op jit(solution)/shard_map/all_gather | solution.py:29
  7.9 140.0 %all-gather.5.cloned.1.call-start = ((), (), s32[]{:S(2)}) async-start(), calls=%async_computation.1 | async-start | bytes 9437184 | tf_op jit(solution)/shard_map/all_gather | solution.py:20
  11.0 136.9 %copy-start = (bf16[512,1024]{1,0:T(8,128)(2,1)S(1)}, bf16[512,1024]{1,0:T(8,128)(2,1)}, u32[]{:S(2)}) copy-start(bf16[512,1024]{1,0:T(8,128)(2,1)} %param.2) | copy-start | bytes 3145732
Sparse Core Ops, SparseCore 0:
  9.6 83.4 all-gather.2
  95.0 52.9 all-gather.4
where the time goes:
time: 213 us; the launch traced here: 212 us
  waiting for transfers between devices  135 us (63%)
  blocking collectives  39.6 us (19%)
  between operations  16.7 us (8%)
  matrix products  11.1 us (5%)
  local copies, waits for them, and re-layouts  5.88 us (3%)
  other arithmetic  4.4 us (2%)
    all_gather x1, waiting for transfers between devices, body(): lax.all_gather(density, 'col', axis=1, tiled=True)  78.5 us
    all_gather x1, waiting for transfers between devices, body(): column_panel = lax.all_gather(density, 'row', axis=0, tiled=True)  54.8 us
    psum x1, blocking collectives, body(): trace_p, trace_c = lax.psum((trace_p_part, trace_c_part), ('row', 'col'))  39.6 us
    dot_general x1, matrix products, body(): jnp.dot(lax.all_gather(density, 'col', axis=1, tiled=True), column_panel,...  11.1 us
  transfers between devices with their start and end apart: 2, of which 2 were waited for; matrix products, arithmetic and copies ran while one was open for 3% of the time, Pallas kernels for 0%

commit v1 on v0

--- a/solution.py
+++ b/solution.py
@@ -4,6 +4,22 @@
 from jax.sharding import PartitionSpec as P
 
 BLK = 64
+
+
+def collect(x, axis, dim):
+    ways, here, step = (lax.axis_size(axis), lax.axis_index(axis), x.shape[dim])
+    dims = [n * ways if d == dim else n for d, n in enumerate(x.shape)]
+    full = lax.dynamic_update_slice_in_dim(jnp.zeros(dims, x.dtype), x, here * step, axis=dim)
+    going_up = going_down = x
+    for far in range(1, ways // 2 + 1):
+        going_up = lax.ppermute(going_up, axis, [(d, (d + 1) % ways) for d in range(ways)])
+        full = lax.dynamic_update_slice_in_dim(full, going_up, (here - far) % ways * step, axis=dim)
+        if 2 * far < ways:
+            going_down = lax.ppermute(going_down, axis, [(d, (d - 1) % ways) for d in range(ways)])
+            full = lax.dynamic_update_slice_in_dim(
+                full, going_down, (here + far) % ways * step, axis=dim
+            )
+    return full
 
 
 def expand_blocks(block_mask, width):
@@ -25,11 +41,7 @@
     on_diagonal = global_rows[:, None] == global_cols[None, :]
     density_wide = density.astype(jnp.float32)
     trace_p_part = jnp.sum(jnp.where(on_diagonal, density_wide, 0.0))
-    square = jnp.dot(
-        lax.all_gather(density, "col", axis=1, tiled=True),
-        column_panel,
-        preferred_element_type=jnp.float32,
-    )
+    square = jnp.dot(collect(density, "col", 1), column_panel, preferred_element_type=jnp.float32)
     square = square * cell_mask
     trace_c_part = jnp.sum(jnp.where(on_diagonal, square, 0.0))
     trace_p, trace_c = lax.psum((trace_p_part, trace_c_part), ("row", "col"))

time: 213 us -> 148 us (0.69)
  waiting for transfers between devices: 135 us -> 53.7 us
  local copies, waits for them, and re-layouts: 5.88 us -> 17 us
  starting transfers between devices: 0.08 us -> 5.21 us
    all_gather x1 -> x0, waiting for transfers between devices: 78.5 us -> none  [body(): lax.all_gather(density, 'col', axis=1, tiled=True)]
    all_gather x1, waiting for transfers between devices: 54.8 us -> 0.01 us  [body(): column_panel = lax.all_gather(density, 'row', axis=0, tiled=True)]
    ppermute x0 -> x3, waiting for transfers between devices: none -> 53 us  [the longest x2 44.9 us: collect(): lax.ppermute(going_up, axis, [(d, (d + 1) % ways) for d in range(ways)])]
    dynamic_update_slice x0 -> x4, local copies, waits for them, and re-layouts: none -> 8.11 us  [the longest x2 4.68 us: collect(): lax.dynamic_update_slice_in_dim(full, going_up, (here - far) % ways * ste...]
    ppermute x0 -> x3, starting transfers between devices: none -> 5.17 us  [the longest x2 3.08 us: collect(): lax.ppermute(going_up, axis, [(d, (d + 1) % ways) for d in range(ways)])]
    broadcast_in_dim x0 -> x1, local copies, waits for them, and re-layouts: none -> 2.48 us  [collect(): jnp.zeros(dims, x.dtype)]
  transfers between devices with their start and end apart: 2 -> 4, of which waited for: 2 -> 3; matrix products, arithmetic and copies ran while one was open for 3% -> 12% of each run, Pallas kernels for 0% -> 0%
where the time goes in v1:
time: 148 us; the launch traced here: 147 us
  waiting for transfers between devices  53.7 us (36%)
  blocking collectives  38.8 us (26%)
  local copies, waits for them, and re-layouts  17 us (11%)
  between operations  16.5 us (11%)
  matrix products  11.1 us (8%)
  starting transfers between devices  5.21 us (4%)
  other arithmetic  5.01 us (3%)
    ppermute x2, waiting for transfers between devices, collect(): lax.ppermute(going_up, axis, [(d, (d + 1) % ways) for d in range(ways)])  44.9 us
    psum x1, blocking collectives, body(): trace_p, trace_c = lax.psum((trace_p_part, trace_c_part), ('row', 'col'))  38.8 us
    dot_general x1, matrix products, body(): jnp.dot(collect(density, 'col', 1), column_panel, preferred_element_type=...  11.1 us
    ppermute x1, waiting for transfers between devices, collect(): lax.ppermute(going_down, axis, [(d, (d - 1) % ways) for d in range(ways)])  8.13 us
    dynamic_update_slice x2, local copies, waits for them, and re-layouts, collect(): lax.dynamic_update_slice_in_dim(full, going_up, (here - far) % ways * ste...  4.68 us
    reshape x1, local copies, waits for them, and re-layouts, expand_blocks(): return grid.reshape(block_rows * width, block_cols * width)  4.1 us
    convert_element_type x1, other arithmetic, body(): return (updated.astype(jnp.bfloat16), occupations)  3.17 us
    ppermute x2, starting transfers between devices, collect(): lax.ppermute(going_up, axis, [(d, (d + 1) % ways) for d in range(ways)])  3.08 us
  transfers between devices with their start and end apart: 4, of which 3 were waited for; matrix products, arithmetic and copies ran while one was open for 12% of the time, Pallas kernels for 0%

profile of v1, /device:TPU:0, one launch (start us, length us, event | category | flops | bytes accessed | tf_op | source)
XLA Modules:
  0.0 147.3 jit_solution(14228139046654437082)
XLA Ops:
  7.2 0.0 all-gather.2.cloned.1.call-start
  7.2 0.7 all-gather.2.cloned.1.call-update
  7.9 3.1 %collective-permute-start = (bf16[512,1024]{1,0:T(8,128)(2,1)}, bf16[512,1024]{1,0:T(8,128)(2,1)}, u32[]{:S(2)}, u32[]{:S(2)}) collective-permute-start(bf16[512,1024]{1,0:T(8,128)(2,1)} %param.2), channel_id=1, source_target_pairs={{0,1},{1,2},{2,3},{3,0},{4,5},{5,6},{6,7},{7,4},{8,9},{9,10},{10,1... | collective-permute-start | bytes 3145736 | tf_op jit(solution)/shard_map/ppermute | solution.py:15
  11.0 2.1 %collective-permute-start.1 = (bf16[512,1024]{1,0:T(8,128)(2,1)}, bf16[512,1024]{1,0:T(8,128)(2,1)}, u32[]{:S(2)}, u32[]{:S(2)}) collective-permute-start(bf16[512,1024]{1,0:T(8,128)(2,1)} %param.2), channel_id=1, source_target_pairs={{0,3},{1,0},{2,1},{3,2},{4,7},{5,4},{6,5},{7,6},{8,11},{9,8},{10,9... | collective-permute-start | bytes 3145736 | tf_op jit(solution)/shard_map/ppermute | solution.py:18
  13.1 24.3 %collective-permute-done = bf16[512,1024]{1,0:T(8,128)(2,1)} collective-permute-done((bf16[512,1024]{1,0:T(8,128)(2,1)}, bf16[512,1024]{1,0:T(8,128)(2,1)}, u32[]{:S(2)}, u32[]{:S(2)}) %collective-permute-start) | collective-permute-done | bytes 1048608 | tf_op jit(solution)/shard_map/ppermute | solution.py:15
  37.4 0.0 collective-permute-start.2
  37.4 0.7 convert_element_type.10
  38.0 2.3 %broadcast_in_dim.18 = f32[8,64,16,64]{3,2,1,0:T(8,128)} broadcast(f32[8,16]{1,0:T(8,128)S(1)} %convert_element_type.10), dimensions={0,2} | broadcast | bytes 2097664 | tf_op jit(solution)/shard_map/broadcast_in_dim | solution.py:27
  40.4 0.0 copy-start
  40.4 4.1 %reshape.16 = f32[512,1024]{1,0:T(8,128)S(1)} reshape(f32[8,64,16,64]{3,2,1,0:T(8,128)} %broadcast_in_dim.18) | data formatting | bytes 4194304 | tf_op jit(solution)/shard_map/reshape | solution.py:30
  44.5 2.5 %broadcast_in_dim.17 = bf16[512,4096]{1,0:T(8,128)(2,1)} broadcast(bf16[]{:T(256)} %constant.46.clone.1), dimensions={} | broadcast | bytes 4194306 | tf_op jit(solution)/shard_map/broadcast_in_dim | solution.py:12
  47.0 0.0 copy-done
  47.0 1.1 constant_dynamic-update-slice_fusion.3
  48.1 2.3 %constant_dynamic-update-slice_fusion.2 = bf16[512,4096]{1,0:T(8,128)(2,1)} fusion(bf16[512,4096]{1,0:T(8,128)(2,1)} %constant_dynamic-update-slice_fusion.3, bf16[512,1024]{1,0:T(8,128)(2,1)} %collective-permute-done, s32[]{:T(128)S(6)} %select_n.50), kind=kLoop, calls=%fused_computation.13 | loop fusion | bytes 2097156 | tf_op jit(solution)/shard_map/dynamic_update_slice | solution.py:16
  50.5 8.1 %collective-permute-done.1 = bf16[512,1024]{1,0:T(8,128)(2,1)} collective-permute-done((bf16[512,1024]{1,0:T(8,128)(2,1)}, bf16[512,1024]{1,0:T(8,128)(2,1)}, u32[]{:S(2)}, u32[]{:S(2)}) %collective-permute-start.1) | collective-permute-done | bytes 1048608 | tf_op jit(solution)/shard_map/ppermute | solution.py:18
  58.6 2.3 %constant_dynamic-update-slice_fusion.1 = bf16[512,4096]{1,0:T(8,128)(2,1)} fusion(bf16[512,4096]{1,0:T(8,128)(2,1)} %constant_dynamic-update-slice_fusion.2, bf16[512,1024]{1,0:T(8,128)(2,1)} %collective-permute-done.1, s32[]{:T(128)S(6)} %select_n.52), kind=kLoop, calls=%fused_computation.12 | loop fusion | bytes 2097156 | tf_op jit(solution)/shard_map/dynamic_update_slice | solution.py:19
  60.9 20.6 %collective-permute-done.2 = bf16[512,1024]{1,0:T(8,128)(2,1)} collective-permute-done((bf16[512,1024]{1,0:T(8,128)(2,1)}, bf16[512,1024]{1,0:T(8,128)(2,1)}, u32[]{:S(2)}, u32[]{:S(2)}) %collective-permute-start.2) | collective-permute-done | bytes 1048608 | tf_op jit(solution)/shard_map/ppermute | solution.py:15
  81.5 2.4 %constant_dynamic-update-slice_fusion = bf16[512,4096]{1,0:T(8,128)(2,1)} fusion(bf16[512,4096]{1,0:T(8,128)(2,1)} %constant_dynamic-update-slice_fusion.1, bf16[512,1024]{1,0:T(8,128)(2,1)} %collective-permute-done.2, s32[]{:T(128)S(6)} %select_n.54), kind=kLoop, calls=%fused_computation.11 | loop fusion | bytes 2097156 | tf_op jit(solution)/shard_map/dynamic_update_slice | solution.py:16
  83.8 0.0 all-gather.2.cloned.1.call-done
  83.8 11.1 %fusion.5 = (f32[]{:T(128)}, f32[]{:T(128)}, f32[512,1024]{1,0:T(8,128)}) fusion(f32[512,1024]{1,0:T(8,128)S(1)} %reshape.16, s32[1024]{0:T(1024)S(1)} %iota_add_fusion, s32[512]{0:T(512)S(1)} %iota_add_fusion.1, bf16[512,1024]{1,0:T(8,128)(2,1)S(1)} %copy-done, bf16[512,4096]{1,0:T(8,128)(2,1)} %constant_dynamic-update-slice_fusion, ...), kind=kOutput, calls=%fused_computation.8 | convolution fusion | flops 4298637312 | bytes 17831944 | tf_op jit(solution)/shard_map/dot_general | solution.py:44
  94.9 38.8 %all-reduce = (f32[]{:T(128)}, f32[]{:T(128)}) all-reduce(f32[]{:T(128)} %get-tuple-element.3, f32[]{:T(128)} %get-tuple-element.2), channel_id=1, replica_groups=mesh['row'=8,'col'=4] {'row','col'}, use_global_device_ids=true, to_apply=%region_1.2 | all-reduce | flops 2 | bytes 16 | tf_op jit(solution)/shard_map/psum | solution.py:47
  136.2 3.2 %fusion.3 = bf16[512,1024]{1,0:T(8,128)(2,1)} fusion(f32[512,1024]{1,0:T(8,128)S(1)} %reshape.16, bf16[512,1024]{1,0:T(8,128)(2,1)S(1)} %copy-done, f32[512,1024]{1,0:T(8,128)} %get-tuple-element.6, pred[]{:T(512)S(6)} %gt.3), kind=kLoop, calls=%fused_computation.6 | loop fusion | flops 3670016 | bytes 6291457 | tf_op jit(solution)/shard_map/convert_element_type | solution.py:53
  139.3 1.1 maximum_multiply_fusion
  (2 shorter events, 0.0 us)
Async XLA Ops:
  7.2 76.7 %all-gather.2.cloned.1.call-start = ((), (), s32[]{:S(2)}) async-start(), calls=%async_computation | async-start | bytes 9437184 | tf_op jit(solution)/shard_map/all_gather | solution.py:36
  7.9 29.5 %collective-permute-start = (bf16[512,1024]{1,0:T(8,128)(2,1)}, bf16[512,1024]{1,0:T(8,128)(2,1)}, u32[]{:S(2)}, u32[]{:S(2)}) collective-permute-start(bf16[512,1024]{1,0:T(8,128)(2,1)} %param.2), channel_id=1, source_target_pairs={{0,1},{1,2},{2,3},{3,0},{4,5},{5,6},{6,7},{7,4},{8,9},{9,10},{10,1... | collective-permute-start | bytes 3145736 | tf_op jit(solution)/shard_map/ppermute | solution.py:15
  11.0 47.6 %collective-permute-start.1 = (bf16[512,1024]{1,0:T(8,128)(2,1)}, bf16[512,1024]{1,0:T(8,128)(2,1)}, u32[]{:S(2)}, u32[]{:S(2)}) collective-permute-start(bf16[512,1024]{1,0:T(8,128)(2,1)} %param.2), channel_id=1, source_target_pairs={{0,3},{1,0},{2,1},{3,2},{4,7},{5,4},{6,5},{7,6},{8,11},{9,8},{10,9... | collective-permute-start | bytes 3145736 | tf_op jit(solution)/shard_map/ppermute | solution.py:18
  37.4 44.1 %collective-permute-start.2 = (bf16[512,1024]{1,0:T(8,128)(2,1)}, bf16[512,1024]{1,0:T(8,128)(2,1)}, u32[]{:S(2)}, u32[]{:S(2)}) collective-permute-start(bf16[512,1024]{1,0:T(8,128)(2,1)} %collective-permute-done), channel_id=1, source_target_pairs={{0,1},{1,2},{2,3},{3,0},{4,5},{5,6},{6,7},{7,4},{8,9},{9,10},{10,1... | collective-permute-start | bytes 3145736 | tf_op jit(solution)/shard_map/ppermute | solution.py:15
  40.4 6.6 %copy-start = (bf16[512,1024]{1,0:T(8,128)(2,1)S(1)}, bf16[512,1024]{1,0:T(8,128)(2,1)}, u32[]{:S(2)}) copy-start(bf16[512,1024]{1,0:T(8,128)(2,1)} %param.2) | copy-start | bytes 3145732
Sparse Core Ops, SparseCore 0:
  9.9 57.0 all-gather.1

commit v2 on v0

--- a/solution.py
+++ b/solution.py
@@ -32,7 +32,7 @@
     )
     square = square * cell_mask
     trace_c_part = jnp.sum(jnp.where(on_diagonal, square, 0.0))
-    trace_p, trace_c = lax.psum((trace_p_part, trace_c_part), ("row", "col"))
+    trace_p, trace_c = lax.psum(lax.psum((trace_p_part, trace_c_part), "col"), "row")
     order_total = slab_rows * lax.axis_size("row")
     take_square = trace_p > 1.0 * order_total
     updated = jnp.where(take_square, square, cell_mask * (2.0 * density_wide - square))

time: 213 us -> 198 us (0.930)
  blocking collectives: 39.6 us -> 24.8 us
    psum x1 -> x2, blocking collectives: 39.6 us -> 24.8 us  [the longest x1 12.5 us: body(): lax.psum(lax.psum((trace_p_part, trace_c_part), 'col'), 'row')]
where the time goes in v2:
time: 198 us
  waiting for transfers between devices  135 us (68%)
  blocking collectives  24.8 us (13%)
  between operations  16.8 us (8%)
  matrix products  11.1 us (6%)
  local copies, waits for them, and re-layouts  5.89 us (3%)
  other arithmetic  4.45 us (2%)
    all_gather x1, waiting for transfers between devices, body(): lax.all_gather(density, 'col', axis=1, tiled=True)  78.5 us
    all_gather x1, waiting for transfers between devices, body(): column_panel = lax.all_gather(density, 'row', axis=0, tiled=True)  54.8 us
    psum x1, blocking collectives, body(): lax.psum(lax.psum((trace_p_part, trace_c_part), 'col'), 'row')  12.5 us
    psum x1, blocking collectives, body(): lax.psum((trace_p_part, trace_c_part), 'col')  12.3 us
    dot_general x1, matrix products, body(): jnp.dot(lax.all_gather(density, 'col', axis=1, tiled=True), column_panel,...  11.1 us
  transfers between devices with their start and end apart: 2, of which 2 were waited for; matrix products, arithmetic and copies ran while one was open for 3% of the time, Pallas kernels for 0%

profile of v2, /device:TPU:0, one launch (start us, length us, event | category | flops | bytes accessed | tf_op | source)
XLA Modules:
  0.0 197.8 jit_solution(15971748451290700694)
XLA Ops:
  7.2 0.0 copy-start.1
  7.2 0.0 all-gather.3.cloned.1.call-start
  7.2 0.7 all-gather.3.cloned.1.call-update
  7.9 0.0 all-gather.5.cloned.1.call-start
  8.0 0.7 all-gather.5.cloned.1.call-update
  8.7 0.0 copy-done.1
  8.7 2.3 %broadcast_in_dim.14 = f32[8,64,16,64]{3,2,1,0:T(8,128)} broadcast(f32[8,16]{1,0:T(8,128)S(1)} %convert_element_type.10), dimensions={0,2} | broadcast | bytes 2097664 | tf_op jit(solution)/shard_map/broadcast_in_dim | solution.py:11
  11.0 0.0 copy-start
  11.0 3.6 %reshape.16 = f32[512,1024]{1,0:T(8,128)S(1)} reshape(f32[8,64,16,64]{3,2,1,0:T(8,128)} %broadcast_in_dim.14) | data formatting | bytes 4194304 | tf_op jit(solution)/shard_map/reshape | solution.py:14
  14.6 78.5 %all-gather.3.cloned.1.call-done = bf16[512,4096]{1,0:T(8,128)(2,1)} async-done(((bf16[512,1024]{1,0:T(8,128)(2,1)}), bf16[512,4096]{1,0:T(8,128)(2,1)}) %all-gather.3.cloned.1.call-update) | async-done | bytes 4194320 | tf_op jit(solution)/shard_map/all_gather | solution.py:29
  93.1 54.8 %all-gather.5.cloned.1.call-done = bf16[4096,1024]{1,0:T(8,128)(2,1)} async-done(((bf16[512,1024]{1,0:T(8,128)(2,1)}), bf16[4096,1024]{1,0:T(8,128)(2,1)}) %all-gather.5.cloned.1.call-update) | async-done | bytes 8388624 | tf_op jit(solution)/shard_map/all_gather | solution.py:20
  147.9 0.0 copy-done
  147.9 11.1 %fusion.5 = (f32[]{:T(128)}, f32[]{:T(128)}, f32[512,1024]{1,0:T(8,128)}) fusion(f32[512,1024]{1,0:T(8,128)S(1)} %reshape.16, s32[1024]{0:T(1024)S(1)} %iota_add_fusion, s32[512]{0:T(512)S(1)} %iota_add_fusion.1, bf16[512,1024]{1,0:T(8,128)(2,1)S(1)} %copy-done, bf16[512,4096]{1,0:T(8,128)(2,1)} %all-gather.3.cloned.1.call-done, ...), kind=kOutput, calls=%fused_computation.8 | convolution fusion | flops 4298637312 | bytes 17831944 | tf_op jit(solution)/shard_map/dot_general | solution.py:28
  159.0 12.3 %all-reduce.1 = (f32[]{:T(128)}, f32[]{:T(128)}) all-reduce(f32[]{:T(128)} %get-tuple-element.3, f32[]{:T(128)} %get-tuple-element.2), channel_id=1, replica_groups=mesh['row'=8,'col'=4] {'col'}, use_global_device_ids=true, to_apply=%region_1.2 | all-reduce | flops 2 | bytes 16 | tf_op jit(solution)/shard_map/psum | solution.py:35
  171.3 12.5 %all-reduce = (f32[]{:T(128)}, f32[]{:T(128)}) all-reduce(f32[]{:T(128)} %get-tuple-element.6, f32[]{:T(128)} %get-tuple-element.7), channel_id=1, replica_groups=mesh['row'=8,'col'=4] {'row'}, use_global_device_ids=true, to_apply=%region_2.3 | all-reduce | flops 2 | bytes 16 | tf_op jit(solution)/shard_map/psum | solution.py:35
  186.5 3.2 %fusion.3 = bf16[512,1024]{1,0:T(8,128)(2,1)} fusion(f32[512,1024]{1,0:T(8,128)S(1)} %reshape.16, bf16[512,1024]{1,0:T(8,128)(2,1)S(1)} %copy-done, f32[512,1024]{1,0:T(8,128)} %get-tuple-element.8, pred[]{:T(512)S(6)} %gt.3), kind=kLoop, calls=%fused_computation.6 | loop fusion | flops 3670016 | bytes 6291457 | tf_op jit(solution)/shard_map/convert_element_type | solution.py:41
  189.7 1.3 maximum_multiply_fusion
  (3 shorter events, 0.0 us)
Async XLA Ops:
  7.2 1.5 copy-start.1
  7.2 85.9 %all-gather.3.cloned.1.call-start = ((), (), s32[]{:S(2)}) async-start(), calls=%async_computation | async-start | bytes 5242880 | tf_op jit(solution)/shard_map/all_gather | solution.py:29
  7.9 140.0 %all-gather.5.cloned.1.call-start = ((), (), s32[]{:S(2)}) async-start(), calls=%async_computation.1 | async-start | bytes 9437184 | tf_op jit(solution)/shard_map/all_gather | solution.py:20
  11.0 136.9 %copy-start = (bf16[512,1024]{1,0:T(8,128)(2,1)S(1)}, bf16[512,1024]{1,0:T(8,128)(2,1)}, u32[]{:S(2)}) copy-start(bf16[512,1024]{1,0:T(8,128)(2,1)} %param.2) | copy-start | bytes 3145732
Sparse Core Ops, SparseCore 0:
  9.6 83.4 all-gather.2
  95.0 52.9 all-gather.4
